TPU v7x, 256 devices: a whole 4x4x8 slice. The times are simulated.
256 devices in a mesh: req: 64 (over z, x, core), tp: 4 (over y).
Axes of the slice: x: 4, y: 4, z: 8, core: 2. Of those that a mesh axis runs over, the one named last changes fastest.
Arguments:
- patches: bfloat16 [65536, 1408], P('req')
- segment_ids: int32 [65536], P('req'), may hold values from 0 to 15, as said below
- grid_sides: int32 [65536], P('req'), may hold values from 8 to 32, as said below
- split_plan: int32 [64, 2], P('req'), may hold values from 0 to 960, as said below
- owner_dev: int32 [16384], P('req'), may hold values from 0 to 63, as said below
- dest_row: int32 [16384], P('req'), may hold values from 0 to 255, as said below
- ln_gain: float32 [1408], replicated, may hold values from 0.25 to 1.75
- ln_bias: float32 [1408], replicated, may hold values from -3 to 3
- w_qkv: bfloat16 [3, 1408, 1408], P(None, 'tp')
- w_out: bfloat16 [1408, 1408], P('tp'), may hold values from -0.625 to 0.625
- w_proj: bfloat16 [5632, 2048], P(None, 'tp'), may hold values from -0.078125 to 0.078125
Outputs:
- vision_tokens: bfloat16 [16384, 2048], P('req', 'tp')
Inputs may be any that keep to these rules, and one draw needn't show every extreme that they name: `segment_ids`: within each packed row the ids start at 0, never fall, and one id's patches are contiguous; an image with grid side s has s * s patches (the last image of the whole packing may be cut short) and lies in at most two neighbouring rows. `grid_sides`: all patches of one image share its grid side, a multiple of 8. split_plan[r, 0] is the number of patches of row r's first image that lie in row r - 1, split_plan[r, 1] the number of patches of row r's last image that lie in row r + 1; both are 0 where no image crosses. `owner_dev`: the merged tokens of one row form blocks of 8 consecutive merged tokens; each block goes whole to one owner, a row's blocks go to different owners, and every owner receives 1024 // 4 merged tokens. `dest_row`: every row of every owner's output receives exactly one merged token.
All inputs are finite; a program needn't handle non-finite values.
Results may differ from a plain program's by a relative error of at most 0.019.
Values may be sent and summed in bfloat16 or wider, within the bound.
No kernel may reach another device: no remote copies, remote signals or barrier semaphores. Data moves between devices by JAX's collectives and lax.ppermute only.
A program may use at most 128 MiB of HBM per device.

v0:
```python
import jax
import jax.numpy as jnp
from jax import lax
from jax.sharding import PartitionSpec as P

HD = 88


def extended(value, sides, width):
    for axis, dim in sides:
        count, length = (lax.axis_size(axis), value.shape[dim])
        up = [(i, (i + 1) % count) for i in range(count - 1)]
        down = [(j, i) for i, j in up]
        last = lax.slice_in_dim(value, length - width, length, axis=dim)
        leading = lax.slice_in_dim(value, 0, width, axis=dim)
        before = lax.ppermute(last, axis, up)
        after = lax.ppermute(leading, axis, down)
        value = jnp.concatenate([before, value, after], axis=dim)
    return value


def layer_norm(inputs, scale_vec, shift_vec):
    widened = inputs.astype(jnp.float32)
    centred = widened - jnp.mean(widened, axis=-1, keepdims=True)
    variance = jnp.mean(centred * centred, axis=-1, keepdims=True)
    return (centred * lax.rsqrt(variance + 1e-06) * scale_vec + shift_vec).astype(jnp.bfloat16)


def grid_positions(seg_row, side_row, first_offset):
    row_len = seg_row.shape[0]
    tok_index = jnp.arange(row_len, dtype=jnp.int32)
    boundary = jnp.concatenate([jnp.ones((1,), dtype=bool), seg_row[1:] != seg_row[:-1]])
    seg_start = lax.cummax(jnp.where(boundary, tok_index, 0), axis=0)
    offset = tok_index - seg_start + jnp.where(seg_row == 0, first_offset, 0)
    half_side = side_row // 2
    window = offset // 4
    corner = offset % 4
    return (2 * (window // half_side) + corner // 2, 2 * (window % half_side) + corner % 2)


def key_labels(seg_row, plan_row):
    row_len = seg_row.shape[0]
    tok_index = jnp.arange(row_len, dtype=jnp.int32)
    before = jnp.where(tok_index >= row_len - plan_row[0], 0, -1).astype(jnp.int32)
    after_keys = jnp.where(tok_index < plan_row[1], seg_row[row_len - 1], -1)
    return jnp.concatenate([before, seg_row, after_keys])


def rotate_pairs(channels, angles, axis_pos):
    quarter = channels.shape[axis_pos] // 2
    first_half = lax.slice_in_dim(channels, 0, quarter, axis=axis_pos)
    second_half = lax.slice_in_dim(channels, quarter, 2 * quarter, axis=axis_pos)
    cosine = jnp.cos(angles)
    sine_tab = jnp.sin(angles)
    return jnp.concatenate(
        [
            first_half * cosine - second_half * sine_tab,
            second_half * cosine + first_half * sine_tab,
        ],
        axis=axis_pos,
    )


def apply_rope(channels, row_angles, col_angles, axis_pos):
    half_width = channels.shape[axis_pos] // 2
    row_part = rotate_pairs(
        lax.slice_in_dim(channels, 0, half_width, axis=axis_pos), row_angles, axis_pos
    )
    col_part = rotate_pairs(
        lax.slice_in_dim(channels, half_width, 2 * half_width, axis=axis_pos), col_angles, axis_pos
    )
    return jnp.concatenate([row_part, col_part], axis=axis_pos)


def on_device(
    patches,
    segment_ids,
    grid_sides,
    split_plan,
    owner_dev,
    dest_row,
    ln_gain,
    ln_bias,
    w_qkv,
    w_out,
    w_proj,
):
    tok_count = patches.shape[0]
    feat_width = patches.shape[1]
    local_width = w_qkv.shape[1]
    local_heads = local_width // HD
    normed = layer_norm(patches, ln_gain, ln_bias)
    mixed_qkv = jnp.einsum("td,kcd->kct", normed, w_qkv, preferred_element_type=jnp.float32)
    grid_row, grid_col = grid_positions(segment_ids, grid_sides, split_plan[0, 0])
    quarter = HD // 4
    frequency = 10000.0 ** (-jnp.arange(quarter, dtype=jnp.float32) / quarter)
    row_angles = frequency[:, None] * grid_row.astype(jnp.float32)[None, :]
    col_angles = frequency[:, None] * grid_col.astype(jnp.float32)[None, :]
    shaped = mixed_qkv.reshape(3, local_heads, HD, tok_count)
    queries = apply_rope(shaped[0], row_angles, col_angles, 1).astype(jnp.bfloat16)
    key_rot = apply_rope(shaped[1], row_angles, col_angles, 1)
    key_value = jnp.stack([key_rot, shaped[2]]).astype(jnp.bfloat16)
    near_kv = extended(key_value, (("req", 3),), tok_count)
    near_keys = near_kv[0]
    near_values = near_kv[1]
    labels = key_labels(segment_ids, split_plan[0])
    block_rows = min(512, tok_count)
    w_heads = w_out.reshape(local_heads, HD, feat_width)

    def attend_block(first_row):
        q_block = lax.dynamic_slice_in_dim(queries, first_row, block_rows, 2)
        seg_block = lax.dynamic_slice_in_dim(segment_ids, first_row, block_rows, 0)
        allowed = seg_block[:, None] == labels[None, :]
        scores = jnp.einsum(
            "hcq,hck->hqk", q_block, near_keys, preferred_element_type=jnp.float32
        ) * HD ** (-0.5)
        scores = jnp.where(allowed[None], scores, -1e30)
        largest = jnp.max(scores, axis=-1, keepdims=True)
        weights = jnp.exp(scores - largest)
        attn_probs = (weights / jnp.sum(weights, axis=-1, keepdims=True)).astype(jnp.bfloat16)
        heads_out = jnp.einsum(
            "hqk,hck->hcq", attn_probs, near_values, preferred_element_type=jnp.float32
        ).astype(jnp.bfloat16)
        return jnp.einsum("hcq,hcd->qd", heads_out, w_heads, preferred_element_type=jnp.float32)

    block_starts = jnp.arange(tok_count // block_rows, dtype=jnp.int32) * block_rows
    partial_value = lax.map(attend_block, block_starts).reshape(tok_count, feat_width)
    attn_sum = lax.psum(partial_value.astype(jnp.bfloat16), "tp").astype(jnp.float32)
    mixed_rows = (patches.astype(jnp.float32) + attn_sum).astype(jnp.bfloat16)
    merged = mixed_rows.reshape(tok_count // 4, 4 * feat_width)
    projected = jnp.dot(merged, w_proj, preferred_element_type=jnp.float32).astype(jnp.bfloat16)
    per_owner = owner_dev.shape[0]
    peer_count = lax.axis_size("req")
    owner_slots = 2 * per_owner // peer_count
    matches = (owner_dev[:, None] == jnp.arange(peer_count, dtype=jnp.int32)[None, :]).astype(
        jnp.int32
    )
    arrival = jnp.sum(jnp.cumsum(matches, axis=0) * matches, axis=1) - 1
    send_slot = owner_dev * owner_slots + arrival
    out_cols = projected.shape[1]
    send_rows = (
        jnp.zeros((peer_count * owner_slots, out_cols), jnp.bfloat16).at[send_slot].set(projected)
    )
    send_dest = (
        jnp.full((peer_count * owner_slots,), per_owner, jnp.int32).at[send_slot].set(dest_row)
    )
    got_rows, got_dest = (
        lax.all_to_all(send_rows, "req", split_axis=0, concat_axis=0, tiled=True),
        lax.all_to_all(send_dest, "req", split_axis=0, concat_axis=0, tiled=True),
    )
    return jnp.zeros((per_owner, out_cols), jnp.bfloat16).at[got_dest].set(got_rows, mode="drop")


def solution(mesh):
    placed = (
        P("req", None),
        P("req"),
        P("req"),
        P("req", None),
        P("req"),
        P("req"),
        P(),
        P(),
        P(None, "tp", None),
        P("tp", None),
        P(None, "tp"),
    )
    return jax.shard_map(
        on_device, mesh=mesh, in_specs=placed, out_specs=P("req", "tp"), check_vma=False
    )
```

profile of v0, /device:TPU:1, one launch (start us, length us, event | category | flops | bytes accessed | tf_op | source)
XLA Modules:
  0.0 257.5 jit_solution(7537347584126004869)
XLA Ops:
  6.6 2.4 convert_reduce_fusion
  9.4 0.9 fusion.26
  10.3 3.8 %fusion.38 = f32[3,352,1024]{2,1,0:T(8,128)S(1)} fusion(bf16[3,352,1408]{2,1,0:T(8,128)(2,1)S(1)} %copy-done, bf16[1024,1408]{1,0:T(8,128)(2,1)S(1)} %copy-done.2, f32[1408]{0:T(1024)S(1)} %copy-done.9, f32[1408]{0:T(1024)S(1)} %copy-done.10, f32[1024]{0:T(1024)S(1)} %add_rsqrt_fusion, f32[1024]{0:T(1024)S(1)} %broadcast_multiply_fusion), kind=kOutput, calls=%fused_computation.42 | convolution fusion | flops 3053715456 | bytes 10202112 | tf_op jit(solution)/shard_map/td,kcd->kct/dot_general | solution.py:93
  14.1 1.4 fusion.72
  18.6 1.8 subtract_convert_fusion.1
  20.5 1.2 pad_maximum_fusion.1
  21.8 4.5 %collective-permute-start = (bf16[2,4,88,1024]{3,2,1,0:T(8,128)(2,1)}, bf16[2,4,88,1024]{3,2,1,0:T(8,128)(2,1)}, u32[]{:S(2)}, u32[]{:S(2)}) collective-permute-start(bf16[2,4,88,1024]{3,2,1,0:T(8,128)(2,1)} %pad_maximum_fusion.1), channel_id=1, source_target_pairs={{0,4},{4,8},{8,12},{12,16},{16,20},{20,24},{24,28},{28,32},{32,36}... | collective-permute-start | bytes 4325384 | tf_op jit(solution)/shard_map/ppermute | solution.py:16
  26.3 3.0 %collective-permute-start.1 = (bf16[2,4,88,1024]{3,2,1,0:T(8,128)(2,1)}, bf16[2,4,88,1024]{3,2,1,0:T(8,128)(2,1)}, u32[]{:S(2)}, u32[]{:S(2)}) collective-permute-start(bf16[2,4,88,1024]{3,2,1,0:T(8,128)(2,1)} %pad_maximum_fusion.1), channel_id=1, source_target_pairs={{4,0},{8,4},{12,8},{16,12},{20,16},{24,20},{28,24},{32,28},{36,32}... | collective-permute-start | bytes 4325384 | tf_op jit(solution)/shard_map/ppermute | solution.py:17
  30.6 1.2 fusion.57
  32.1 1.1 pad_maximum_fusion.2
  33.2 9.4 %collective-permute-done = bf16[2,4,88,1024]{3,2,1,0:T(8,128)(2,1)} collective-permute-done((bf16[2,4,88,1024]{3,2,1,0:T(8,128)(2,1)}, bf16[2,4,88,1024]{3,2,1,0:T(8,128)(2,1)}, u32[]{:S(2)}, u32[]{:S(2)}) %collective-permute-start) | collective-permute-done | bytes 1441824 | tf_op jit(solution)/shard_map/ppermute | solution.py:16
  42.5 4.4 %collective-permute-done.1 = bf16[2,4,88,1024]{3,2,1,0:T(8,128)(2,1)} collective-permute-done((bf16[2,4,88,1024]{3,2,1,0:T(8,128)(2,1)}, bf16[2,4,88,1024]{3,2,1,0:T(8,128)(2,1)}, u32[]{:S(2)}, u32[]{:S(2)}) %collective-permute-start.1) | collective-permute-done | bytes 1441824 | tf_op jit(solution)/shard_map/ppermute | solution.py:17
  46.9 2.0 pad_maximum_fusion
  48.9 2.5 slice_bitcast_fusion
  51.4 69.2 %while.10 = (s32[]{:T(128)}, bf16[2,512,1408]{2,1,0:T(8,128)(2,1)}, s32[2]{0:T(128)S(1)}, s32[1024]{0:T(1024)S(1)}, s32[3072]{0:T(1024)S(1)}, /*index=5*/bf16[4,...) while((s32[]{:T(128)}, bf16[2,512,1408]{2,1,0:T(8,128)(2,1)}, ...), condition=%wide.region_11.12_spmd, body=%wide.region_8.11_spmd.sunk | while | flops 2761608192 | bytes 62073512 | solution.py:127
  54.2 0.9 broadcast_compare_fusion.2
  55.1 15.8 %fusion.91 = (f32[4,512]{1,0:T(4,128)S(1)}, f32[4,512,3072]{2,1,0:T(8,128)}) fusion(pred[512,3072]{1,0:T(8,128)(4,1)S(1)} %broadcast_compare_fusion.2, bf16[4,88,3072]{2,1,0:T(8,128)(2,1)} %get-tuple-element.190, bf16[4,88,1024]{2,1,0:T(8,128)(2,1)S(1)} %get-tuple-element.189, s32[]{:T(128)S(6)} %select_n.147), kind=kOutput, calls=%fused_computation.129.clone.1 | convolution fusion | flops 1132465152 | bytes 29270020 | tf_op jit(solution)/shard_map/while/body/eval_jaxpr/sub | solution.py:119
  70.9 15.1 %fusion.92 = bf16[2,512,1408]{2,1,0:T(8,128)(2,1)} fusion(bf16[2,512,1408]{2,1,0:T(8,128)(2,1)} %get-tuple-element.173, s32[]{:T(128)} %get-tuple-element.172, bf16[4,88,1408]{2,1,0:T(8,128)(2,1)} %get-tuple-element.192, bf16[4,88,3072]{2,1,0:T(8,128)(2,1)} %get-tuple-element.191, f32[4,512,3072]{2,1,0:T(8,128)} %get-tuple-element.158, ...), kind=kOutput, calls=%fused_computation.13.clone.1 | convolution fusion | flops 1627570176 | bytes 31212032 | tf_op jit(solution)/shard_map/while/body/eval_jaxpr/hcq,hcd->qd/dot_general | solution.py:124
  88.8 0.9 broadcast_compare_fusion.2
  89.8 15.8 %fusion.91 = (f32[4,512]{1,0:T(4,128)S(1)}, f32[4,512,3072]{2,1,0:T(8,128)}) fusion(pred[512,3072]{1,0:T(8,128)(4,1)S(1)} %broadcast_compare_fusion.2, bf16[4,88,3072]{2,1,0:T(8,128)(2,1)} %get-tuple-element.190, bf16[4,88,1024]{2,1,0:T(8,128)(2,1)S(1)} %get-tuple-element.189, s32[]{:T(128)S(6)} %select_n.147), kind=kOutput, calls=%fused_computation.129.clone.1 | convolution fusion | flops 1132465152 | bytes 29270020 | tf_op jit(solution)/shard_map/while/body/eval_jaxpr/sub | solution.py:119
  105.6 15.0 %fusion.92 = bf16[2,512,1408]{2,1,0:T(8,128)(2,1)} fusion(bf16[2,512,1408]{2,1,0:T(8,128)(2,1)} %get-tuple-element.173, s32[]{:T(128)} %get-tuple-element.172, bf16[4,88,1408]{2,1,0:T(8,128)(2,1)} %get-tuple-element.192, bf16[4,88,3072]{2,1,0:T(8,128)(2,1)} %get-tuple-element.191, f32[4,512,3072]{2,1,0:T(8,128)} %get-tuple-element.158, ...), kind=kOutput, calls=%fused_computation.13.clone.1 | convolution fusion | flops 1627570176 | bytes 31212032 | tf_op jit(solution)/shard_map/while/body/eval_jaxpr/hcq,hcd->qd/dot_general | solution.py:124
  122.2 1.6 scatter_custom_fusion
  124.5 13.9 %all-to-all-start = ((s32[64,8,1]{1,2,0:T(1,128)}), s32[64,8,1]{1,2,0:T(1,128)S(1)}, u32[]{:S(2)}, u32[]{:S(2)}) async-start(s32[64,8,1]{1,2,0:T(1,128)} %bitcast.6), calls=%async_computation | async-start | bytes 65536 | tf_op jit(solution)/shard_map/all_to_all | solution.py:149
  138.3 63.5 %all-reduce.2.cloned.1.call-done = bf16[1024,1408]{1,0:T(8,128)(2,1)} async-done(((bf16[1024,1408]{1,0:T(8,128)(2,1)}), bf16[1024,1408]{1,0:T(8,128)(2,1)}) %all-reduce.2.cloned.1.call-update) | async-done | bytes 2883600 | tf_op jit(solution)/shard_map/psum | solution.py:128
  201.9 4.1 %fusion.30 = bf16[1024,1408]{1,0:T(8,128)(2,1)} fusion(bf16[1024,1408]{1,0:T(8,128)(2,1)S(1)} %copy-done.3, bf16[1024,1408]{1,0:T(8,128)(2,1)} %all-reduce.2.cloned.1.call-done), kind=kLoop, calls=%fused_computation.34 | loop fusion | flops 5767168 | bytes 8650752 | tf_op jit(solution)/shard_map/convert_element_type | solution.py:129
  206.0 5.6 %reshape.244 = bf16[256,5632]{1,0:T(8,128)(2,1)} reshape(bf16[1024,1408]{1,0:T(8,128)(2,1)} %fusion.30) | data formatting | bytes 5767168 | tf_op jit(solution)/shard_map/reshape | solution.py:130
  211.6 5.3 %convolution_convert_fusion = bf16[256,512]{1,0:T(8,128)(2,1)S(1)} fusion(bf16[256,5632]{1,0:T(8,128)(2,1)} %reshape.244, bf16[5632,512]{1,0:T(8,128)(2,1)} %param.23), kind=kOutput, calls=%fused_computation.47 | convolution fusion | flops 1476526080 | bytes 8912896 | tf_op jit(solution)/shard_map/dot_general | solution.py:131
  216.9 2.3 scatter_custom_fusion.1
  219.3 10.7 %all-to-all-start.1 = ((bf16[64,8,512]{2,1,0:T(8,128)(2,1)}), bf16[64,8,512]{2,1,0:T(8,128)(2,1)S(1)}, u32[]{:S(2)}, u32[]{:S(2)}) async-start(bf16[64,8,512]{2,1,0:T(8,128)(2,1)} %bitcast.23), calls=%async_computation.1 | async-start | bytes 1048576 | tf_op jit(solution)/shard_map/all_to_all | solution.py:148
  230.5 1.4 reduce.7
  232.8 14.9 %all-to-all-done.1 = bf16[64,8,512]{2,1,0:T(8,128)(2,1)S(1)} async-done(((bf16[64,8,512]{2,1,0:T(8,128)(2,1)}), bf16[64,8,512]{2,1,0:T(8,128)(2,1)S(1)}, u32[]{:S(2)}, u32[]{:S(2)}) %all-to-all-start.1) | async-done | bytes 524320 | tf_op jit(solution)/shard_map/all_to_all | solution.py:148
  247.6 3.0 %scatter_custom_fusion.2 = bf16[256,512]{1,0:T(8,128)(2,1)} fusion(s32[512]{0:T(512)S(1)} %bitcast.91, bf16[64,8,512]{2,1,0:T(8,128)(2,1)S(1)} %all-to-all-done.1, bf16[]{:T(256)} %constant.105.clone.1), kind=kCustom, calls=%fused_computation.50 | custom fusion | bytes 786434 | tf_op jit(solution)/shard_map/scatter | solution.py:151
  (59 shorter events, 9.7 us)
Async XLA Ops:
  6.5 3.7 %copy-start = (bf16[3,352,1408]{2,1,0:T(8,128)(2,1)S(1)}, bf16[3,352,1408]{2,1,0:T(8,128)(2,1)}, u32[]{:S(2)}) copy-start(bf16[3,352,1408]{2,1,0:T(8,128)(2,1)} %param.21) | copy-start | bytes 8921092
  6.5 195.3 %all-reduce.2.cloned.1.call-start = ((), (), s32[]{:S(2)}) async-start(), calls=%async_computation.2 | async-start | bytes 5767168 | tf_op jit(solution)/shard_map/psum | solution.py:128
  6.5 2.8 %copy-start.2 = (bf16[1024,1408]{1,0:T(8,128)(2,1)S(1)}, bf16[1024,1408]{1,0:T(8,128)(2,1)}, u32[]{:S(2)}) copy-start(bf16[1024,1408]{1,0:T(8,128)(2,1)} %param.13) | copy-start | bytes 8650756
  6.6 3.7 %copy-start.9 = (f32[1408]{0:T(1024)S(1)}, f32[1408]{0:T(1024)}, u32[]{:S(2)}) copy-start(f32[1408]{0:T(1024)} %param.20) | copy-start | bytes 16900
  6.6 3.7 %copy-start.10 = (f32[1408]{0:T(1024)S(1)}, f32[1408]{0:T(1024)}, u32[]{:S(2)}) copy-start(f32[1408]{0:T(1024)} %param.19) | copy-start | bytes 16900
  14.1 1.5 copy-start.8
  14.1 2.1 copy-start.5
  14.1 2.8 %copy-start.7 = (s32[1024]{0:T(1024)S(1)}, s32[1024]{0:T(1024)}, u32[]{:S(2)}) copy-start(s32[1024]{0:T(1024)} %param.15) | copy-start | bytes 12292
  21.8 20.8 %collective-permute-start = (bf16[2,4,88,1024]{3,2,1,0:T(8,128)(2,1)}, bf16[2,4,88,1024]{3,2,1,0:T(8,128)(2,1)}, u32[]{:S(2)}, u32[]{:S(2)}) collective-permute-start(bf16[2,4,88,1024]{3,2,1,0:T(8,128)(2,1)} %pad_maximum_fusion.1), channel_id=1, source_target_pairs={{0,4},{4,8},{8,12},{12,16},{16,20},{20,24},{24,28},{28,32},{32,36}... | collective-permute-start | bytes 4325384 | tf_op jit(solution)/shard_map/ppermute | solution.py:16
  26.3 20.6 %collective-permute-start.1 = (bf16[2,4,88,1024]{3,2,1,0:T(8,128)(2,1)}, bf16[2,4,88,1024]{3,2,1,0:T(8,128)(2,1)}, u32[]{:S(2)}, u32[]{:S(2)}) collective-permute-start(bf16[2,4,88,1024]{3,2,1,0:T(8,128)(2,1)} %pad_maximum_fusion.1), channel_id=1, source_target_pairs={{4,0},{8,4},{12,8},{16,12},{20,16},{24,20},{28,24},{32,28},{36,32}... | collective-permute-start | bytes 4325384 | tf_op jit(solution)/shard_map/ppermute | solution.py:17
  48.9 2.5 copy-start.4
  120.5 0.7 copy-start.6
  120.6 81.3 %copy-start.3 = (bf16[1024,1408]{1,0:T(8,128)(2,1)S(1)}, bf16[1024,1408]{1,0:T(8,128)(2,1)}, u32[]{:S(2)}) copy-start(bf16[1024,1408]{1,0:T(8,128)(2,1)} %param.13) | copy-start | bytes 8650756
  124.5 94.8 %all-to-all-start = ((s32[64,8,1]{1,2,0:T(1,128)}), s32[64,8,1]{1,2,0:T(1,128)S(1)}, u32[]{:S(2)}, u32[]{:S(2)}) async-start(s32[64,8,1]{1,2,0:T(1,128)} %bitcast.6), calls=%async_computation | async-start | bytes 65536 | tf_op jit(solution)/shard_map/all_to_all | solution.py:149
  211.6 39.0 %copy-start.1 = (bf16[3,352,1408]{2,1,0:T(8,128)(2,1)S(1)}, bf16[3,352,1408]{2,1,0:T(8,128)(2,1)}, u32[]{:S(2)}) copy-start(bf16[3,352,1408]{2,1,0:T(8,128)(2,1)} %param.21) | copy-start | bytes 8921092
  219.3 28.4 %all-to-all-start.1 = ((bf16[64,8,512]{2,1,0:T(8,128)(2,1)}), bf16[64,8,512]{2,1,0:T(8,128)(2,1)S(1)}, u32[]{:S(2)}, u32[]{:S(2)}) async-start(bf16[64,8,512]{2,1,0:T(8,128)(2,1)} %bitcast.23), calls=%async_computation.1 | async-start | bytes 1048576 | tf_op jit(solution)/shard_map/all_to_all | solution.py:148
Sparse Core Ops, SparseCore 0:
  120.7 81.1 all-reduce.1
where the time goes:
time: 258 us
  waiting for transfers between devices  92.2 us (36%)
  matrix products  70.8 us (27%)
  starting transfers between devices  32 us (12%)
  local copies, waits for them, and re-layouts  22.7 us (9%)
  other arithmetic  21.3 us (8%)
  between operations  14.3 us (6%)
  loops' own time  4.17 us (2%)
    psum x1, waiting for transfers between devices, on_device(): lax.psum(partial_value.astype(jnp.bfloat16), 'tp').astype(jnp.float32)  63.5 us
    sub x2, matrix products, attend_block(): weights = jnp.exp(scores - largest)  31.7 us
    dot_general x2, matrix products, attend_block(): jnp.einsum('hcq,hcd->qd', heads_out, w_heads, preferred_element_type=jnp....  30.1 us
    all_to_all x1, waiting for transfers between devices, on_device(): lax.all_to_all(send_rows, 'req', split_axis=0, concat_axis=0, tiled=True)  14.9 us
    all_to_all x1, starting transfers between devices, on_device(): lax.all_to_all(send_dest, 'req', split_axis=0, concat_axis=0, tiled=True)  13.9 us
    all_to_all x1, starting transfers between devices, on_device(): lax.all_to_all(send_rows, 'req', split_axis=0, concat_axis=0, tiled=True)  10.7 us
    ppermute x1, waiting for transfers between devices, extended(): before = lax.ppermute(last, axis, up)  9.36 us
    reshape x1, local copies, waits for them, and re-layouts, on_device(): merged = mixed_rows.reshape(tok_count // 4, 4 * feat_width)  5.62 us
  transfers between devices with their start and end apart: 5, of which 4 were waited for; matrix products, arithmetic and copies ran while one was open for 10% of the time, Pallas kernels for 0%

commit v1 on v0

--- a/solution.py
+++ b/solution.py
@@ -125,7 +125,8 @@
 
     block_starts = jnp.arange(tok_count // block_rows, dtype=jnp.int32) * block_rows
     partial_value = lax.map(attend_block, block_starts).reshape(tok_count, feat_width)
-    attn_sum = lax.psum(partial_value.astype(jnp.bfloat16), "tp").astype(jnp.float32)
+    part_lane_here = lambda point: lax.all_gather(point, axis_name="tp").sum(axis=0)
+    attn_sum = part_lane_here(partial_value.astype(jnp.bfloat16)).astype(jnp.float32)
     mixed_rows = (patches.astype(jnp.float32) + attn_sum).astype(jnp.bfloat16)
     merged = mixed_rows.reshape(tok_count // 4, 4 * feat_width)
     projected = jnp.dot(merged, w_proj, preferred_element_type=jnp.float32).astype(jnp.bfloat16)

time: 258 us -> 302 us (1.17)
  waiting for transfers between devices: 92.2 us -> 129 us
  other arithmetic: 21.3 us -> 28.9 us
    all_gather x0 -> x1, waiting for transfers between devices: none -> 99.2 us  [on_device(): lax.all_gather(point, axis_name='tp').sum(axis=0)]
    psum x1 -> x0, waiting for transfers between devices: 63.5 us -> none  [on_device(): lax.psum(partial_value.astype(jnp.bfloat16), 'tp').astype(jnp.float32)]
    reduce_sum x0 -> x1, other arithmetic: none -> 8.43 us  [on_device(): lax.all_gather(point, axis_name='tp').sum(axis=0)]
  transfers between devices with their start and end apart: 5 -> 5, of which waited for: 4 -> 4; matrix products, arithmetic and copies ran while one was open for 10% -> 11% of each run, Pallas kernels for 0% -> 0%
where the time goes in v1:
time: 302 us
  waiting for transfers between devices  129 us (43%)
  matrix products  70.8 us (23%)
  starting transfers between devices  32 us (11%)
  other arithmetic  28.9 us (10%)
  local copies, waits for them, and re-layouts  22.7 us (8%)
  between operations  14.3 us (5%)
  loops' own time  4.17 us (1%)
    all_gather x1, waiting for transfers between devices, on_device(): lax.all_gather(point, axis_name='tp').sum(axis=0)  99.2 us
    sub x2, matrix products, attend_block(): weights = jnp.exp(scores - largest)  31.7 us
    dot_general x2, matrix products, attend_block(): jnp.einsum('hcq,hcd->qd', heads_out, w_heads, preferred_element_type=jnp....  30.1 us
    all_to_all x1, waiting for transfers between devices, on_device(): lax.all_to_all(send_rows, 'req', split_axis=0, concat_axis=0, tiled=True)  14.9 us
    all_to_all x1, starting transfers between devices, on_device(): lax.all_to_all(send_dest, 'req', split_axis=0, concat_axis=0, tiled=True)  13.9 us
    all_to_all x1, starting transfers between devices, on_device(): lax.all_to_all(send_rows, 'req', split_axis=0, concat_axis=0, tiled=True)  10.7 us
    ppermute x1, waiting for transfers between devices, extended(): before = lax.ppermute(last, axis, up)  10.2 us
    reduce_sum x1, other arithmetic, on_device(): lax.all_gather(point, axis_name='tp').sum(axis=0)  8.43 us
  transfers between devices with their start and end apart: 5, of which 4 were waited for; matrix products, arithmetic and copies ran while one was open for 11% of the time, Pallas kernels for 0%

profile of v1, /device:TPU:1, one launch (start us, length us, event | category | flops | bytes accessed | tf_op | source)
XLA Modules:
  0.0 301.7 jit_solution(14051829650097646454)
XLA Ops:
  6.6 2.4 convert_reduce_fusion
  9.4 0.9 fusion.26
  10.3 3.8 %fusion.38 = f32[3,352,1024]{2,1,0:T(8,128)S(1)} fusion(bf16[3,352,1408]{2,1,0:T(8,128)(2,1)S(1)} %copy-done, bf16[1024,1408]{1,0:T(8,128)(2,1)S(1)} %copy-done.2, f32[1408]{0:T(1024)S(1)} %copy-done.8, f32[1408]{0:T(1024)S(1)} %copy-done.9, f32[1024]{0:T(1024)S(1)} %add_rsqrt_fusion, f32[1024]{0:T(1024)S(1)} %broadcast_multiply_fusion), kind=kOutput, calls=%fused_computation.42 | convolution fusion | flops 3053715456 | bytes 10202112 | tf_op jit(solution)/shard_map/td,kcd->kct/dot_general | solution.py:93
  14.1 1.4 fusion.72
  18.6 1.8 subtract_convert_fusion.1
  20.5 1.2 pad_maximum_fusion.1
  21.8 4.5 %collective-permute-start = (bf16[2,4,88,1024]{3,2,1,0:T(8,128)(2,1)}, bf16[2,4,88,1024]{3,2,1,0:T(8,128)(2,1)}, u32[]{:S(2)}, u32[]{:S(2)}) collective-permute-start(bf16[2,4,88,1024]{3,2,1,0:T(8,128)(2,1)} %pad_maximum_fusion.1), channel_id=1, source_target_pairs={{0,4},{4,8},{8,12},{12,16},{16,20},{20,24},{24,28},{28,32},{32,36}... | collective-permute-start | bytes 4325384 | tf_op jit(solution)/shard_map/ppermute | solution.py:16
  26.3 3.0 %collective-permute-start.1 = (bf16[2,4,88,1024]{3,2,1,0:T(8,128)(2,1)}, bf16[2,4,88,1024]{3,2,1,0:T(8,128)(2,1)}, u32[]{:S(2)}, u32[]{:S(2)}) collective-permute-start(bf16[2,4,88,1024]{3,2,1,0:T(8,128)(2,1)} %pad_maximum_fusion.1), channel_id=1, source_target_pairs={{4,0},{8,4},{12,8},{16,12},{20,16},{24,20},{28,24},{32,28},{36,32}... | collective-permute-start | bytes 4325384 | tf_op jit(solution)/shard_map/ppermute | solution.py:17
  30.6 1.2 fusion.57
  32.3 10.2 %collective-permute-done = bf16[2,4,88,1024]{3,2,1,0:T(8,128)(2,1)} collective-permute-done((bf16[2,4,88,1024]{3,2,1,0:T(8,128)(2,1)}, bf16[2,4,88,1024]{3,2,1,0:T(8,128)(2,1)}, u32[]{:S(2)}, u32[]{:S(2)}) %collective-permute-start) | collective-permute-done | bytes 1441824 | tf_op jit(solution)/shard_map/ppermute | solution.py:16
  42.5 4.4 %collective-permute-done.1 = bf16[2,4,88,1024]{3,2,1,0:T(8,128)(2,1)} collective-permute-done((bf16[2,4,88,1024]{3,2,1,0:T(8,128)(2,1)}, bf16[2,4,88,1024]{3,2,1,0:T(8,128)(2,1)}, u32[]{:S(2)}, u32[]{:S(2)}) %collective-permute-start.1) | collective-permute-done | bytes 1441824 | tf_op jit(solution)/shard_map/ppermute | solution.py:17
  46.9 2.0 pad_maximum_fusion
  48.9 2.5 slice_bitcast_fusion
  51.3 69.2 %while.10 = (s32[]{:T(128)}, bf16[2,512,1408]{2,1,0:T(8,128)(2,1)}, s32[2]{0:T(128)S(1)}, s32[1024]{0:T(1024)S(1)}, s32[3072]{0:T(1024)S(1)}, /*index=5*/bf16[4,...) while((s32[]{:T(128)}, bf16[2,512,1408]{2,1,0:T(8,128)(2,1)}, ...), condition=%wide.region_11.12_spmd, body=%wide.region_8.11_spmd.sunk | while | flops 2761608192 | bytes 62073512 | solution.py:127
  54.2 0.9 broadcast_compare_fusion.2
  55.1 15.8 %fusion.91 = (f32[4,512]{1,0:T(4,128)S(1)}, f32[4,512,3072]{2,1,0:T(8,128)}) fusion(pred[512,3072]{1,0:T(8,128)(4,1)S(1)} %broadcast_compare_fusion.2, bf16[4,88,3072]{2,1,0:T(8,128)(2,1)} %get-tuple-element.190, bf16[4,88,1024]{2,1,0:T(8,128)(2,1)S(1)} %get-tuple-element.189, s32[]{:T(128)S(6)} %select_n.147), kind=kOutput, calls=%fused_computation.129.clone.1 | convolution fusion | flops 1132465152 | bytes 29270020 | tf_op jit(solution)/shard_map/while/body/eval_jaxpr/sub | solution.py:119
  70.9 15.1 %fusion.92 = bf16[2,512,1408]{2,1,0:T(8,128)(2,1)} fusion(bf16[2,512,1408]{2,1,0:T(8,128)(2,1)} %get-tuple-element.173, s32[]{:T(128)} %get-tuple-element.172, bf16[4,88,1408]{2,1,0:T(8,128)(2,1)} %get-tuple-element.192, bf16[4,88,3072]{2,1,0:T(8,128)(2,1)} %get-tuple-element.191, f32[4,512,3072]{2,1,0:T(8,128)} %get-tuple-element.158, ...), kind=kOutput, calls=%fused_computation.13.clone.1 | convolution fusion | flops 1627570176 | bytes 31212032 | tf_op jit(solution)/shard_map/while/body/eval_jaxpr/hcq,hcd->qd/dot_general | solution.py:124
  88.8 0.9 broadcast_compare_fusion.2
  89.7 15.8 %fusion.91 = (f32[4,512]{1,0:T(4,128)S(1)}, f32[4,512,3072]{2,1,0:T(8,128)}) fusion(pred[512,3072]{1,0:T(8,128)(4,1)S(1)} %broadcast_compare_fusion.2, bf16[4,88,3072]{2,1,0:T(8,128)(2,1)} %get-tuple-element.190, bf16[4,88,1024]{2,1,0:T(8,128)(2,1)S(1)} %get-tuple-element.189, s32[]{:T(128)S(6)} %select_n.147), kind=kOutput, calls=%fused_computation.129.clone.1 | convolution fusion | flops 1132465152 | bytes 29270020 | tf_op jit(solution)/shard_map/while/body/eval_jaxpr/sub | solution.py:119
  105.6 15.0 %fusion.92 = bf16[2,512,1408]{2,1,0:T(8,128)(2,1)} fusion(bf16[2,512,1408]{2,1,0:T(8,128)(2,1)} %get-tuple-element.173, s32[]{:T(128)} %get-tuple-element.172, bf16[4,88,1408]{2,1,0:T(8,128)(2,1)} %get-tuple-element.192, bf16[4,88,3072]{2,1,0:T(8,128)(2,1)} %get-tuple-element.191, f32[4,512,3072]{2,1,0:T(8,128)} %get-tuple-element.158, ...), kind=kOutput, calls=%fused_computation.13.clone.1 | convolution fusion | flops 1627570176 | bytes 31212032 | tf_op jit(solution)/shard_map/while/body/eval_jaxpr/hcq,hcd->qd/dot_general | solution.py:124
  122.2 1.6 scatter_custom_fusion
  124.5 13.9 %all-to-all-start = ((s32[64,8,1]{1,2,0:T(1,128)}), s32[64,8,1]{1,2,0:T(1,128)S(1)}, u32[]{:S(2)}, u32[]{:S(2)}) async-start(s32[64,8,1]{1,2,0:T(1,128)} %bitcast.6), calls=%async_computation | async-start | bytes 65536 | tf_op jit(solution)/shard_map/all_to_all | solution.py:150
  138.4 99.2 %all-gather.2.cloned.1.call-done = bf16[4,1024,1408]{2,1,0:T(8,128)(2,1)} async-done(((bf16[1,1024,1408]{2,1,0:T(8,128)(2,1)}), bf16[4,1024,1408]{2,1,0:T(8,128)(2,1)}) %all-gather.2.cloned.1.call-update) | async-done | bytes 11534352 | tf_op jit(solution)/shard_map/all_gather | solution.py:128
  237.5 8.4 %reduce_sum.51 = bf16[1024,1408]{1,0:T(8,128)(2,1)} reduce(bf16[4,1024,1408]{2,1,0:T(8,128)(2,1)} %all-gather.2.cloned.1.call-done, bf16[]{:T(256)} %constant.106.clone.1), dimensions={0}, to_apply=%region_12.13 | reduce | flops 4325376 | bytes 14417922 | tf_op jit(solution)/shard_map/reduce_sum | solution.py:128
  246.0 4.2 %fusion.30 = bf16[1024,1408]{1,0:T(8,128)(2,1)} fusion(bf16[1024,1408]{1,0:T(8,128)(2,1)S(1)} %copy-done.3, bf16[1024,1408]{1,0:T(8,128)(2,1)} %reduce_sum.51), kind=kLoop, calls=%fused_computation.34 | loop fusion | flops 5767168 | bytes 8650752 | tf_op jit(solution)/shard_map/convert_element_type | solution.py:130
  250.2 5.6 %reshape.254 = bf16[256,5632]{1,0:T(8,128)(2,1)} reshape(bf16[1024,1408]{1,0:T(8,128)(2,1)} %fusion.30) | data formatting | bytes 5767168 | tf_op jit(solution)/shard_map/reshape | solution.py:131
  255.8 5.3 %convolution_convert_fusion = bf16[256,512]{1,0:T(8,128)(2,1)S(1)} fusion(bf16[256,5632]{1,0:T(8,128)(2,1)} %reshape.254, bf16[5632,512]{1,0:T(8,128)(2,1)} %param.23), kind=kOutput, calls=%fused_computation.47 | convolution fusion | flops 1476526080 | bytes 8912896 | tf_op jit(solution)/shard_map/dot_general | solution.py:132
  261.1 2.3 scatter_custom_fusion.1
  263.4 10.7 %all-to-all-start.1 = ((bf16[64,8,512]{2,1,0:T(8,128)(2,1)}), bf16[64,8,512]{2,1,0:T(8,128)(2,1)S(1)}, u32[]{:S(2)}, u32[]{:S(2)}) async-start(bf16[64,8,512]{2,1,0:T(8,128)(2,1)} %bitcast.23), calls=%async_computation.1 | async-start | bytes 1048576 | tf_op jit(solution)/shard_map/all_to_all | solution.py:149
  274.7 1.4 reduce.8
  276.9 14.9 %all-to-all-done.1 = bf16[64,8,512]{2,1,0:T(8,128)(2,1)S(1)} async-done(((bf16[64,8,512]{2,1,0:T(8,128)(2,1)}), bf16[64,8,512]{2,1,0:T(8,128)(2,1)S(1)}, u32[]{:S(2)}, u32[]{:S(2)}) %all-to-all-start.1) | async-done | bytes 524320 | tf_op jit(solution)/shard_map/all_to_all | solution.py:149
  291.8 3.0 %scatter_custom_fusion.2 = bf16[256,512]{1,0:T(8,128)(2,1)} fusion(s32[512]{0:T(512)S(1)} %bitcast.91, bf16[64,8,512]{2,1,0:T(8,128)(2,1)S(1)} %all-to-all-done.1, bf16[]{:T(256)} %constant.106.clone.1), kind=kCustom, calls=%fused_computation.50 | custom fusion | bytes 786434 | tf_op jit(solution)/shard_map/scatter | solution.py:152
  (58 shorter events, 9.9 us)
Async XLA Ops:
  6.5 3.7 %copy-start = (bf16[3,352,1408]{2,1,0:T(8,128)(2,1)S(1)}, bf16[3,352,1408]{2,1,0:T(8,128)(2,1)}, u32[]{:S(2)}) copy-start(bf16[3,352,1408]{2,1,0:T(8,128)(2,1)} %param.21) | copy-start | bytes 8921092
  6.5 231.0 %all-gather.2.cloned.1.call-start = ((), (), s32[]{:S(2)}) async-start(), calls=%async_computation.2 | async-start | bytes 14417920 | tf_op jit(solution)/shard_map/all_gather | solution.py:128
  6.5 2.8 copy-start.2
  6.6 3.7 %copy-start.8 = (f32[1408]{0:T(1024)S(1)}, f32[1408]{0:T(1024)}, u32[]{:S(2)}) copy-start(f32[1408]{0:T(1024)} %param.20) | copy-start | bytes 16900
  6.6 3.7 %copy-start.9 = (f32[1408]{0:T(1024)S(1)}, f32[1408]{0:T(1024)}, u32[]{:S(2)}) copy-start(f32[1408]{0:T(1024)} %param.19) | copy-start | bytes 16900
  14.1 1.5 copy-start.7
  14.1 2.1 copy-start.4
  14.1 2.8 copy-start.6
  21.8 20.8 %collective-permute-start = (bf16[2,4,88,1024]{3,2,1,0:T(8,128)(2,1)}, bf16[2,4,88,1024]{3,2,1,0:T(8,128)(2,1)}, u32[]{:S(2)}, u32[]{:S(2)}) collective-permute-start(bf16[2,4,88,1024]{3,2,1,0:T(8,128)(2,1)} %pad_maximum_fusion.1), channel_id=1, source_target_pairs={{0,4},{4,8},{8,12},{12,16},{16,20},{20,24},{24,28},{28,32},{32,36}... | collective-permute-start | bytes 4325384 | tf_op jit(solution)/shard_map/ppermute | solution.py:16
  26.3 20.6 %collective-permute-start.1 = (bf16[2,4,88,1024]{3,2,1,0:T(8,128)(2,1)}, bf16[2,4,88,1024]{3,2,1,0:T(8,128)(2,1)}, u32[]{:S(2)}, u32[]{:S(2)}) collective-permute-start(bf16[2,4,88,1024]{3,2,1,0:T(8,128)(2,1)} %pad_maximum_fusion.1), channel_id=1, source_target_pairs={{4,0},{8,4},{12,8},{16,12},{20,16},{24,20},{28,24},{32,28},{36,32}... | collective-permute-start | bytes 4325384 | tf_op jit(solution)/shard_map/ppermute | solution.py:17
  120.6 0.7 copy-start.5
  124.5 138.9 %all-to-all-start = ((s32[64,8,1]{1,2,0:T(1,128)}), s32[64,8,1]{1,2,0:T(1,128)S(1)}, u32[]{:S(2)}, u32[]{:S(2)}) async-start(s32[64,8,1]{1,2,0:T(1,128)} %bitcast.6), calls=%async_computation | async-start | bytes 65536 | tf_op jit(solution)/shard_map/all_to_all | solution.py:150
  138.3 107.6 %copy-start.3 = (bf16[1024,1408]{1,0:T(8,128)(2,1)S(1)}, bf16[1024,1408]{1,0:T(8,128)(2,1)}, u32[]{:S(2)}) copy-start(bf16[1024,1408]{1,0:T(8,128)(2,1)} %param.13) | copy-start | bytes 8650756
  255.8 39.0 %copy-start.1 = (bf16[3,352,1408]{2,1,0:T(8,128)(2,1)S(1)}, bf16[3,352,1408]{2,1,0:T(8,128)(2,1)}, u32[]{:S(2)}) copy-start(bf16[3,352,1408]{2,1,0:T(8,128)(2,1)} %param.21) | copy-start | bytes 8921092
  263.4 28.4 %all-to-all-start.1 = ((bf16[64,8,512]{2,1,0:T(8,128)(2,1)}), bf16[64,8,512]{2,1,0:T(8,128)(2,1)S(1)}, u32[]{:S(2)}, u32[]{:S(2)}) async-start(bf16[64,8,512]{2,1,0:T(8,128)(2,1)} %bitcast.23), calls=%async_computation.1 | async-start | bytes 1048576 | tf_op jit(solution)/shard_map/all_to_all | solution.py:149
Sparse Core Ops, SparseCore 0:
  120.7 116.7 all-gather.1
